TPU v7x, 256 devices: a whole 4x4x8 slice. The times are simulated.
256 devices in a mesh: row: 8 (over z_hi, y), col: 16 (over x, z_lo), rep: 2 (over core).
Axes of the slice: x: 4, y: 4, z: 8 (z_hi: 2, z_lo: 4; z = z_hi * 4 + z_lo), core: 2. Of those that a mesh axis runs over, the one named last changes fastest.
Arguments:
- ancestor_inverse: float32 [16384, 16384], P('row', 'col'), may hold values from -6 to 6
- tile_structure: int32 [128, 128], P('row', 'col'), may hold values from 0 to 1, as said below
- factor: float32 [16384, 512], P(('row', 'col')), may hold values from -0.046875 to 0.046875
- factor_normalizer: float32 [512, 512], replicated, may hold values from -1 to 1, as said below
- pivot_inverse: float32 [512, 512], P(None, 'rep'), may hold values from -6 to 6, as said below
Outputs:
- ancestor_columns: float32 [16384, 512], P(('row', 'col'), 'rep')
- diag_block: float32 [512, 512], P(None, 'rep')
Inputs may be any that keep to these rules, and one draw needn't show every extreme that they name: `tile_structure`: symmetric, with ones on the diagonal. `factor_normalizer`: lower triangular with ones on its diagonal. `pivot_inverse`: symmetric.
All inputs are finite; a program needn't handle non-finite values.
Results may differ from a plain program's by a relative error of at most 0.000078.
Values sent between devices are 32-bit elements; how exact they have to be, the bound alone decides.
A program may use at most 64 MiB of HBM per device.

v0:
```python
import jax
import jax.numpy as jnp
from jax import lax
from jax.sharding import PartitionSpec as P


def spread(block, axis, owner):
    block = jnp.where(lax.axis_index(axis) == owner, block, jnp.zeros_like(block))
    return lax.psum(block, axis)


def partner(block, axis, distance):
    count = lax.axis_size(axis)
    route = []
    for low in range(count):
        high = low | 1 << distance
        if high != low and high < count:
            route += [(low, high), (high, low)]
    return lax.ppermute(block, axis, route)


def contract_rows(left, right):
    return lax.dot_general(
        left,
        right,
        (((0,), (0,)), ((), ())),
        precision=lax.Precision.HIGHEST,
        preferred_element_type=jnp.float32,
    )


def body(ancestor_inverse, tile_structure, factor, factor_normalizer, pivot_inverse):
    tile_rows = factor.shape[0]
    half_width = pivot_inverse.shape[1]
    copy_index = lax.axis_index("rep")
    column_index = lax.axis_index("col")
    row_count = lax.axis_size("row")
    column_count = lax.axis_size("col")
    column_ratio = column_count // row_count
    block_rows = tile_rows * row_count
    normed = jnp.dot(
        factor,
        factor_normalizer,
        precision=lax.Precision.HIGHEST,
        preferred_element_type=jnp.float32,
    )
    own_columns = lax.dynamic_slice_in_dim(normed, copy_index * half_width, half_width, 1)
    gathered = lax.all_gather(own_columns, "col", axis=0, tiled=True)
    shared = spread(gathered, "row", column_index // column_ratio)
    column_block = lax.dynamic_slice_in_dim(
        shared, column_index % column_ratio * block_rows, block_rows, 0
    )
    tile_marks = tile_structure.astype(jnp.float32)
    across = ancestor_inverse.shape[1] // tile_rows
    masked = (
        ancestor_inverse.reshape(
            tile_rows * lax.axis_size("col") // tile_rows, tile_rows, across, tile_rows
        )
        * tile_marks[:, None, :, None]
    ).reshape(tile_rows * lax.axis_size("col"), across * tile_rows)
    ancestor_columns = lax.psum_scatter(
        -jnp.dot(
            masked,
            column_block,
            precision=lax.Precision.HIGHEST,
            preferred_element_type=jnp.float32,
        ),
        "col",
        scatter_dimension=0,
        tiled=True,
    )
    coupling_term = contract_rows(normed, ancestor_columns)
    coupling = lax.psum(coupling_term, ("row", "col"))
    outgoing_rows = lax.dynamic_slice_in_dim(coupling, (1 - copy_index) * half_width, half_width, 0)
    incoming = partner(outgoing_rows, "rep", 0)
    own_block = lax.dynamic_slice_in_dim(coupling, copy_index * half_width, half_width, 0)
    mirrored = jnp.where(
        copy_index == 0,
        jnp.concatenate([own_block, incoming], 1),
        jnp.concatenate([incoming, own_block], 1),
    )
    diag_block = pivot_inverse - 0.5 * (coupling + mirrored.T)
    return (ancestor_columns, diag_block)


def solution(mesh):
    return jax.shard_map(
        body,
        mesh=mesh,
        in_specs=(P("row", "col"), P("row", "col"), P(("row", "col"), None), P(), P(None, "rep")),
        out_specs=(P(("row", "col"), "rep"), P(None, "rep")),
        check_vma=False,
    )
```

profile of v0, /device:TPU:1, one launch (start us, length us, event | category | flops | bytes accessed | tf_op | source)
XLA Modules:
  0.0 569.2 jit_solution(9534586514955601280)
XLA Ops:
  7.2 0.0 copy-start
  7.2 0.0 all-gather.2.cloned.1.call-start
  7.2 1.2 copy-done
  8.4 1.7 fusion.9
  10.1 0.7 constant_dynamic-slice_fusion.2
  10.7 0.0 all-gather.2.cloned.1.call-update
  10.8 0.0 all-reduce.3.cloned.1.call-start
  10.8 82.3 %all-gather.2.cloned.1.call-done = f32[2048,256]{1,0:T(8,128)} async-done(((f32[128,256]{1,0:T(8,128)}), f32[2048,256]{1,0:T(8,128)}) %all-gather.2.cloned.1.call-update) | async-done | bytes 2097168 | tf_op jit(solution)/shard_map/all_gather | solution.py:48
  93.1 3.1 broadcast_select_fusion
  96.2 0.0 copy-start.4
  96.2 0.0 all-reduce.3.cloned.1.call-update
  96.2 0.0 reduce-scatter.2.cloned.1.call-start
  96.3 0.6 copy-done.4
  96.9 0.1 copy.7
  96.9 138.5 %all-reduce.3.cloned.1.call-done = f32[2048,256]{1,0:T(8,128)} async-done(((f32[2048,256]{1,0:T(8,128)}), f32[2048,256]{1,0:T(8,128)}) %all-reduce.3.cloned.1.call-update) | async-done | bytes 2097168 | tf_op jit(solution)/shard_map/psum | solution.py:9
  235.4 0.0 copy-start.2
  235.4 0.6 mul.27
  236.0 1.0 copy-done.2
  237.0 10.5 %fusion.2 = f32[2048,256]{1,0:T(8,128)} fusion(f32[2048,1024]{1,0:T(8,128)} %param.5, f32[256,8,8,128]{3,2,1,0:T(8,128)S(1)} %bitcast.19, f32[2048,256]{1,0:T(8,128)S(1)} %copy-done.2, s32[]{:T(128)S(6)} %select_n.42), kind=kOutput, calls=%fused_computation.3 | convolution fusion | flops 6445072384 | bytes 19922948 | tf_op jit(solution)/shard_map/dot_general | solution.py:62
  247.5 0.0 reduce-scatter.2.cloned.1.call-update
  247.6 0.0 copy-start.3
  247.6 0.0 all-reduce.5.cloned.1.call-start
  247.6 81.7 %reduce-scatter.2.cloned.1.call-done = f32[128,256]{1,0:T(8,128)} async-done(((f32[2048,256]{1,0:T(8,128)}), f32[128,256]{1,0:T(8,128)}) %reduce-scatter.2.cloned.1.call-update) | async-done | bytes 131088 | tf_op jit(solution)/shard_map/reduce_scatter | solution.py:61
  329.3 2.3 fusion.10
  331.6 0.0 all-reduce.5.cloned.1.call-update
  331.7 222.4 %all-reduce.5.cloned.1.call-done = f32[512,256]{1,0:T(8,128)} async-done(((f32[512,256]{1,0:T(8,128)}), f32[512,256]{1,0:T(8,128)}) %all-reduce.5.cloned.1.call-update) | async-done | bytes 524304 | tf_op jit(solution)/shard_map/psum | solution.py:73
  554.0 0.0 copy-start.1
  554.0 1.1 constant_dynamic-slice_fusion.1
  555.1 0.1 copy.11
  555.3 5.3 collective-permute-start
  560.6 0.1 copy.10
  560.7 1.0 collective-permute-done
  561.7 0.0 copy-done.3
  561.7 0.0 copy-done.1
  561.7 0.9 fusion.7
  (1 shorter events, 0.0 us)
Async XLA Ops:
  7.2 1.2 copy-start
  7.2 85.9 %all-gather.2.cloned.1.call-start = ((), (), s32[]{:S(2)}) async-start(), calls=%async_computation.1 | async-start | bytes 2228224 | tf_op jit(solution)/shard_map/all_gather | solution.py:48
  10.8 224.7 %all-reduce.3.cloned.1.call-start = ((), (), s32[]{:S(2)}) async-start(), calls=%async_computation.2 | async-start | bytes 4194304 | tf_op jit(solution)/shard_map/psum | solution.py:9
  96.2 0.7 copy-start.4
  96.2 233.1 %reduce-scatter.2.cloned.1.call-start = ((), (), s32[]{:S(2)}) async-start(), calls=%async_computation.3 | async-start | bytes 2228224 | tf_op jit(solution)/shard_map/reduce_scatter | solution.py:61
  235.4 1.6 copy-start.2
  247.6 314.2 %copy-start.3 = (f32[512,256]{1,0:T(8,128)S(1)}, f32[512,256]{1,0:T(8,128)}, u32[]{:S(2)}) copy-start(f32[512,256]{1,0:T(8,128)} %param.9) | copy-start | bytes 1572868
  247.6 306.4 %all-reduce.5.cloned.1.call-start = ((), (), s32[]{:S(2)}) async-start(), calls=%async_computation.4 | async-start | bytes 1048576 | tf_op jit(solution)/shard_map/psum | solution.py:73
  554.0 7.7 %copy-start.1 = (f32[512,256]{1,0:T(8,128)S(1)}, f32[512,256]{1,0:T(8,128)}, u32[]{:S(2)}) copy-start(f32[512,256]{1,0:T(8,128)} %all-reduce.5.cloned.1.call-done) | copy-start | bytes 1572868
  555.3 6.4 %collective-permute-start = (f32[256,256]{0,1:T(8,128)S(1)}, f32[256,256]{0,1:T(8,128)S(1)}, u32[]{:S(2)}, u32[]{:S(2)}) collective-permute-start(f32[256,256]{0,1:T(8,128)S(1)} %copy.11), channel_id=1, source_target_pairs={{0,1},{1,0},{2,3},{3,2},{4,5},{5,4},{6,7},{7,6},{8,9},{9,8},{10,11... | collective-permute-start | bytes 786440 | tf_op jit(solution)/shard_map/ppermute | solution.py:19
Sparse Core Ops, SparseCore 0:
  10.9 82.1 all-gather.1
  96.3 139.0 all-reduce.2
  247.7 81.5 reduce-scatter.1
  335.2 218.8 all-reduce.4
where the time goes:
time: 569 us
  waiting for transfers between devices  526 us (92%)
  matrix products  14.5 us (3%)
  between operations  13.9 us (2%)
    psum x1, waiting for transfers between devices, body(): coupling = lax.psum(coupling_term, ('row', 'col'))  222 us
    psum x1, waiting for transfers between devices, spread(): return lax.psum(block, axis)  138 us
    all_gather x1, waiting for transfers between devices, body(): gathered = lax.all_gather(own_columns, 'col', axis=0, tiled=True)  82.3 us
    reduce_scatter x1, waiting for transfers between devices, body(): lax.psum_scatter(-jnp.dot(masked, column_block, precision=lax.Precision.H...  81.7 us
  transfers between devices with their start and end apart: 5, of which 5 were waited for; matrix products, arithmetic and copies ran while one was open for 0% of the time, Pallas kernels for 0%

commit v1 on v0

--- a/solution.py
+++ b/solution.py
@@ -2,11 +2,12 @@
 import jax.numpy as jnp
 from jax import lax
 from jax.sharding import PartitionSpec as P
+from jax.lax import all_gather
 
 
 def spread(block, axis, owner):
     block = jnp.where(lax.axis_index(axis) == owner, block, jnp.zeros_like(block))
-    return lax.psum(block, axis)
+    return all_gather(block, axis_name=axis).sum(axis=0)
 
 
 def partner(block, axis, distance):

time: 569 us -> 745 us (1.31)
  waiting for transfers between devices: 526 us -> 696 us
    all_gather x0 -> x1, waiting for transfers between devices: none -> 314 us  [spread(): return all_gather(block, axis_name=axis).sum(axis=0)]
    psum x1 -> x0, waiting for transfers between devices: 138 us -> none  [spread(): return lax.psum(block, axis)]
where the time goes in v1:
time: 745 us
  waiting for transfers between devices  696 us (93%)
  matrix products  14.5 us (2%)
  between operations  13.9 us (2%)
  other arithmetic  11.1 us (1%)
    all_gather x1, waiting for transfers between devices, spread(): return all_gather(block, axis_name=axis).sum(axis=0)  314 us
    psum x1, waiting for transfers between devices, body(): coupling = lax.psum(coupling_term, ('row', 'col'))  223 us
    all_gather x1, waiting for transfers between devices, body(): gathered = lax.all_gather(own_columns, 'col', axis=0, tiled=True)  82.3 us
    reduce_scatter x1, waiting for transfers between devices, body(): lax.psum_scatter(-jnp.dot(masked, column_block, precision=lax.Precision.H...  76.1 us
  transfers between devices with their start and end apart: 5, of which 5 were waited for; matrix products, arithmetic and copies ran while one was open for 0% of the time, Pallas kernels for 0%

profile of v1, /device:TPU:1, one launch (start us, length us, event | category | flops | bytes accessed | tf_op | source)
XLA Modules:
  0.0 745.1 jit_solution(11564645330830692076)
XLA Ops:
  7.2 0.0 copy-start
  7.2 0.0 all-gather.4.cloned.1.call-start
  7.2 1.2 copy-done
  8.4 1.7 fusion.9
  10.1 0.7 constant_dynamic-slice_fusion.2
  10.7 0.0 all-gather.4.cloned.1.call-update
  10.8 0.0 all-gather.6.cloned.1.call-start
  10.8 82.3 %all-gather.4.cloned.1.call-done = f32[2048,256]{1,0:T(8,128)} async-done(((f32[128,256]{1,0:T(8,128)}), f32[2048,256]{1,0:T(8,128)}) %all-gather.4.cloned.1.call-update) | async-done | bytes 2097168 | tf_op jit(solution)/shard_map/all_gather | solution.py:49
  93.1 3.1 broadcast_select_fusion
  96.2 0.0 copy-start.3
  96.2 0.0 all-gather.6.cloned.1.call-update
  96.2 0.0 reduce-scatter.2.cloned.1.call-start
  96.3 0.6 copy-done.3
  96.9 0.1 copy.7
  96.9 313.6 %all-gather.6.cloned.1.call-done = f32[16384,256]{1,0:T(8,128)} async-done(((f32[2048,256]{1,0:T(8,128)}), f32[16384,256]{1,0:T(8,128)}) %all-gather.6.cloned.1.call-update) | async-done | bytes 16777232 | tf_op jit(solution)/shard_map/all_gather | solution.py:10
  410.5 7.1 reduce_sum.9
  417.7 0.6 mul.27
  418.3 10.5 %fusion.2 = f32[2048,256]{1,0:T(8,128)} fusion(f32[2048,1024]{1,0:T(8,128)} %param.5, f32[256,8,8,128]{3,2,1,0:T(8,128)S(1)} %bitcast.20, f32[2048,256]{1,0:T(8,128)S(1)} %reduce_sum.9, s32[]{:T(128)S(6)} %select_n.42), kind=kOutput, calls=%fused_computation.3 | convolution fusion | flops 6445072384 | bytes 19922948 | tf_op jit(solution)/shard_map/dot_general | solution.py:63
  428.8 0.0 reduce-scatter.2.cloned.1.call-update
  428.8 0.0 copy-start.2
  428.8 0.0 all-reduce.2.cloned.1.call-start
  428.9 76.1 %reduce-scatter.2.cloned.1.call-done = f32[128,256]{1,0:T(8,128)} async-done(((f32[2048,256]{1,0:T(8,128)}), f32[128,256]{1,0:T(8,128)}) %reduce-scatter.2.cloned.1.call-update) | async-done | bytes 131088 | tf_op jit(solution)/shard_map/reduce_scatter | solution.py:62
  504.9 2.3 fusion.10
  507.3 0.0 all-reduce.2.cloned.1.call-update
  507.3 222.6 %all-reduce.2.cloned.1.call-done = f32[512,256]{1,0:T(8,128)} async-done(((f32[512,256]{1,0:T(8,128)}), f32[512,256]{1,0:T(8,128)}) %all-reduce.2.cloned.1.call-update) | async-done | bytes 524304 | tf_op jit(solution)/shard_map/psum | solution.py:74
  729.9 0.0 copy-start.1
  729.9 1.1 constant_dynamic-slice_fusion.1
  731.1 0.1 copy.11
  731.2 5.3 collective-permute-start
  736.5 0.1 copy.10
  736.6 1.0 collective-permute-done
  737.6 0.0 copy-done.2
  737.6 0.0 copy-done.1
  737.6 0.9 fusion.7
  (1 shorter events, 0.0 us)
Async XLA Ops:
  7.2 1.2 copy-start
  7.2 85.9 %all-gather.4.cloned.1.call-start = ((), (), s32[]{:S(2)}) async-start(), calls=%async_computation.1 | async-start | bytes 2228224 | tf_op jit(solution)/shard_map/all_gather | solution.py:49
  10.8 399.8 %all-gather.6.cloned.1.call-start = ((), (), s32[]{:S(2)}) async-start(), calls=%async_computation.4 | async-start | bytes 18874368 | tf_op jit(solution)/shard_map/all_gather | solution.py:10
  96.2 0.7 copy-start.3
  96.2 408.7 %reduce-scatter.2.cloned.1.call-start = ((), (), s32[]{:S(2)}) async-start(), calls=%async_computation.2 | async-start | bytes 2228224 | tf_op jit(solution)/shard_map/reduce_scatter | solution.py:62
  428.8 308.8 %copy-start.2 = (f32[512,256]{1,0:T(8,128)S(1)}, f32[512,256]{1,0:T(8,128)}, u32[]{:S(2)}) copy-start(f32[512,256]{1,0:T(8,128)} %param.9) | copy-start | bytes 1572868
  428.8 301.1 %all-reduce.2.cloned.1.call-start = ((), (), s32[]{:S(2)}) async-start(), calls=%async_computation.3 | async-start | bytes 1048576 | tf_op jit(solution)/shard_map/psum | solution.py:74
  729.9 7.7 %copy-start.1 = (f32[512,256]{1,0:T(8,128)S(1)}, f32[512,256]{1,0:T(8,128)}, u32[]{:S(2)}) copy-start(f32[512,256]{1,0:T(8,128)} %all-reduce.2.cloned.1.call-done) | copy-start | bytes 1572868
  731.2 6.4 collective-permute-start
Sparse Core Ops, SparseCore 0:
  10.9 82.1 all-gather.3
  96.3 314.1 all-gather.5
  428.9 75.9 reduce-scatter.1
  510.8 219.0 all-reduce.1

commit v2 on v0

--- a/solution.py
+++ b/solution.py
@@ -45,7 +45,15 @@
         preferred_element_type=jnp.float32,
     )
     own_columns = lax.dynamic_slice_in_dim(normed, copy_index * half_width, half_width, 1)
-    gathered = lax.all_gather(own_columns, "col", axis=0, tiled=True)
+
+    def edit_orders(array_in):
+        w_next = jnp.stack([array_in for _ in range(lax.psum(1, axis_name="col"))])
+        w2 = jnp.concatenate(
+            lax.all_to_all(w_next, axis_name="col", split_axis=0, concat_axis=0), axis=0
+        )
+        return w2
+
+    gathered = edit_orders(own_columns)
     shared = spread(gathered, "row", column_index // column_ratio)
     column_block = lax.dynamic_slice_in_dim(
         shared, column_index % column_ratio * block_rows, block_rows, 0

time: 569 us -> 538 us (0.946)
  waiting for transfers between devices: 526 us -> 486 us
  starting transfers between devices: 5.44 us -> 14.4 us
    all_gather x1 -> x0, waiting for transfers between devices: 82.3 us -> none  [body(): gathered = lax.all_gather(own_columns, 'col', axis=0, tiled=True)]
    all_to_all x0 -> x1, waiting for transfers between devices: none -> 49.7 us  [edit_orders(): lax.all_to_all(w_next, axis_name='col', split_axis=0, concat_axis=0)]
    all_to_all x0 -> x1, starting transfers between devices: none -> 9.02 us  [edit_orders(): lax.all_to_all(w_next, axis_name='col', split_axis=0, concat_axis=0)]
    psum x1, waiting for transfers between devices: 138 us -> 130 us  [spread(): return lax.psum(block, axis)]
where the time goes in v2:
time: 538 us; the launch traced here: 537 us
  waiting for transfers between devices  486 us (90%)
  matrix products  14.5 us (3%)
  starting transfers between devices  14.4 us (3%)
  between operations  13.9 us (3%)
  local copies, waits for them, and re-layouts  6.42 us (1%)
    psum x1, waiting for transfers between devices, body(): coupling = lax.psum(coupling_term, ('row', 'col'))  223 us
    psum x1, waiting for transfers between devices, spread(): return lax.psum(block, axis)  130 us
    reduce_scatter x1, waiting for transfers between devices, body(): lax.psum_scatter(-jnp.dot(masked, column_block, precision=lax.Precision.H...  81.7 us
    all_to_all x1, waiting for transfers between devices, edit_orders(): lax.all_to_all(w_next, axis_name='col', split_axis=0, concat_axis=0)  49.7 us
  transfers between devices with their start and end apart: 5, of which 5 were waited for; matrix products, arithmetic and copies ran while one was open for 0% of the time, Pallas kernels for 0%

profile of v2, /device:TPU:1, one launch (start us, length us, event | category | flops | bytes accessed | tf_op | source)
XLA Modules:
  0.0 537.3 jit_solution(2869457468529821402)
XLA Ops:
  7.2 0.0 copy-start
  7.2 1.2 copy-done
  8.4 1.7 fusion.9
  10.1 1.5 stack.2
  11.6 9.0 %all-to-all-start = ((f32[16,128,256]{2,1,0:T(8,128)}), f32[16,128,256]{2,1,0:T(8,128)S(1)}, u32[]{:S(2)}, u32[]{:S(2)}) async-start(f32[16,128,256]{2,1,0:T(8,128)} %stack.2), calls=%async_computation | async-start | bytes 4194304 | tf_op jit(solution)/shard_map/all_to_all | solution.py:52
  20.7 0.0 all-reduce.3.cloned.1.call-start
  20.7 49.7 %all-to-all-done = f32[16,128,256]{2,1,0:T(8,128)S(1)} async-done(((f32[16,128,256]{2,1,0:T(8,128)}), f32[16,128,256]{2,1,0:T(8,128)S(1)}, u32[]{:S(2)}, u32[]{:S(2)}) %all-to-all-start) | async-done | bytes 2097184 | tf_op jit(solution)/shard_map/all_to_all | solution.py:52
  70.4 1.6 broadcast_select_fusion
  72.0 0.0 copy-start.4
  72.0 0.0 all-reduce.3.cloned.1.call-update
  72.0 0.0 reduce-scatter.2.cloned.1.call-start
  72.1 0.6 copy-done.4
  72.7 0.1 copy.7
  72.8 130.3 %all-reduce.3.cloned.1.call-done = f32[2048,256]{1,0:T(8,128)} async-done(((f32[2048,256]{1,0:T(8,128)}), f32[2048,256]{1,0:T(8,128)}) %all-reduce.3.cloned.1.call-update) | async-done | bytes 2097168 | tf_op jit(solution)/shard_map/psum | solution.py:9
  203.0 0.0 copy-start.2
  203.0 0.6 mul.27
  203.6 1.0 copy-done.2
  204.6 10.5 %fusion.2 = f32[2048,256]{1,0:T(8,128)} fusion(f32[2048,1024]{1,0:T(8,128)} %param.5, f32[256,8,8,128]{3,2,1,0:T(8,128)S(1)} %bitcast.20, f32[2048,256]{1,0:T(8,128)S(1)} %copy-done.2, s32[]{:T(128)S(6)} %select_n.46), kind=kOutput, calls=%fused_computation.3 | convolution fusion | flops 6445072384 | bytes 19922948 | tf_op jit(solution)/shard_map/dot_general | solution.py:70
  215.2 0.0 reduce-scatter.2.cloned.1.call-update
  215.2 0.0 copy-start.3
  215.2 0.0 all-reduce.5.cloned.1.call-start
  215.2 81.7 %reduce-scatter.2.cloned.1.call-done = f32[128,256]{1,0:T(8,128)} async-done(((f32[2048,256]{1,0:T(8,128)}), f32[128,256]{1,0:T(8,128)}) %reduce-scatter.2.cloned.1.call-update) | async-done | bytes 131088 | tf_op jit(solution)/shard_map/reduce_scatter | solution.py:69
  296.9 2.3 fusion.10
  299.3 0.0 all-reduce.5.cloned.1.call-update
  299.3 222.9 %all-reduce.5.cloned.1.call-done = f32[512,256]{1,0:T(8,128)} async-done(((f32[512,256]{1,0:T(8,128)}), f32[512,256]{1,0:T(8,128)}) %all-reduce.5.cloned.1.call-update) | async-done | bytes 524304 | tf_op jit(solution)/shard_map/psum | solution.py:81
  522.2 0.0 copy-start.1
  522.2 1.1 constant_dynamic-slice_fusion.1
  523.3 0.1 copy.11
  523.4 5.3 collective-permute-start
  528.7 0.1 copy.10
  528.8 1.0 collective-permute-done
  529.9 0.0 copy-done.3
  529.9 0.0 copy-done.1
  529.9 0.9 fusion.7
  (2 shorter events, 0.0 us)
Async XLA Ops:
  7.2 1.2 copy-start
  11.6 58.8 %all-to-all-start = ((f32[16,128,256]{2,1,0:T(8,128)}), f32[16,128,256]{2,1,0:T(8,128)S(1)}, u32[]{:S(2)}, u32[]{:S(2)}) async-start(f32[16,128,256]{2,1,0:T(8,128)} %stack.2), calls=%async_computation | async-start | bytes 4194304 | tf_op jit(solution)/shard_map/all_to_all | solution.py:52
  20.7 182.4 %all-reduce.3.cloned.1.call-start = ((), (), s32[]{:S(2)}) async-start(), calls=%async_computation.2 | async-start | bytes 4194304 | tf_op jit(solution)/shard_map/psum | solution.py:9
  72.0 0.7 copy-start.4
  72.0 224.9 %reduce-scatter.2.cloned.1.call-start = ((), (), s32[]{:S(2)}) async-start(), calls=%async_computation.3 | async-start | bytes 2228224 | tf_op jit(solution)/shard_map/reduce_scatter | solution.py:69
  203.0 1.6 copy-start.2
  215.2 314.7 %copy-start.3 = (f32[512,256]{1,0:T(8,128)S(1)}, f32[512,256]{1,0:T(8,128)}, u32[]{:S(2)}) copy-start(f32[512,256]{1,0:T(8,128)} %param.9) | copy-start | bytes 1572868
  215.2 307.0 %all-reduce.5.cloned.1.call-start = ((), (), s32[]{:S(2)}) async-start(), calls=%async_computation.4 | async-start | bytes 1048576 | tf_op jit(solution)/shard_map/psum | solution.py:81
  522.2 7.7 %copy-start.1 = (f32[512,256]{1,0:T(8,128)S(1)}, f32[512,256]{1,0:T(8,128)}, u32[]{:S(2)}) copy-start(f32[512,256]{1,0:T(8,128)} %all-reduce.5.cloned.1.call-done) | copy-start | bytes 1572868
  523.4 6.4 %collective-permute-start = (f32[256,256]{0,1:T(8,128)S(1)}, f32[256,256]{0,1:T(8,128)S(1)}, u32[]{:S(2)}, u32[]{:S(2)}) collective-permute-start(f32[256,256]{0,1:T(8,128)S(1)} %copy.11), channel_id=1, source_target_pairs={{0,1},{1,0},{2,3},{3,2},{4,5},{5,4},{6,7},{7,6},{8,9},{9,8},{10,11... | collective-permute-start | bytes 786440 | tf_op jit(solution)/shard_map/ppermute | solution.py:19
Sparse Core Ops, SparseCore 0:
  72.2 130.8 all-reduce.2
  215.3 81.5 reduce-scatter.1
  302.9 219.1 all-reduce.4
